TPU v7x, 256 devices: a whole 4x4x8 slice. The times are simulated.
256 devices in a mesh: row: 16 (over x_lo, y, core), col: 16 (over x_hi, z).
Axes of the slice: x: 4 (x_hi: 2, x_lo: 2; x = x_hi * 2 + x_lo), y: 4, z: 8, core: 2. Of those that a mesh axis runs over, the one named last changes fastest.
Arguments:
- slab: float32 [32768, 8192], P('row', 'col'), may hold values from -250 to 250
- sketch_op: float32 [256, 32768], P(None, 'row'), may hold values from -0.03125 to 0.03125
- block_order: int32 [64], replicated, may hold values from 0 to 63, as said below
- pivots: int32 [2, 128], replicated, may hold values from 0 to 8191, as said below
Outputs:
- slab_out: float32 [32768, 8192], P('row', 'col')
- factor_rows: float32 [256, 8192], P(None, 'col')
- sketch_out: float32 [256, 8192], P(None, 'col')
Inputs may be any that keep to these rules, and one draw needn't show every extreme that they name: A permutation of the 64 storage blocks; panel k uses block block_order[k]. `pivots`: each row holds 128 different storage columns, none of them in the storage blocks block_order[0 .. 1].
All inputs are finite; a program needn't handle non-finite values.
Results may differ from a plain program's by a relative error of at most 0.00012.
Values sent between devices are 32-bit elements; how exact they have to be, the bound alone decides.
No kernel may reach another device: no remote copies, remote signals or barrier semaphores. Data moves between devices by JAX's collectives and lax.ppermute only.
A program may use at most 64 MiB of HBM per device.

v0:
```python
import jax
import jax.numpy as jnp
from jax import lax
from jax.sharding import PartitionSpec as P


def from_root(value, axis, source):
    kept = jnp.where(lax.axis_index(axis) == source, value, 0).astype(value.dtype)
    return lax.psum(kept, axis)


def contract_rows(left, right):
    return lax.dot_general(
        left,
        right,
        (((0,), (0,)), ((), ())),
        precision=lax.Precision.HIGHEST,
        preferred_element_type=jnp.float32,
    )


def right_solve(lower_factor, values):
    return lax.linalg.triangular_solve(
        lower_factor, values, left_side=False, lower=True, transpose_a=True
    )


def local(slab, sketch_op, block_order, pivots):
    highest = lax.Precision.HIGHEST
    local_width = slab.shape[1]
    panel_width = pivots.shape[1]
    col_place = lax.axis_index("col")
    col_base = col_place * local_width
    local_cols = col_base + jnp.arange(local_width, dtype=jnp.int32)
    partial_sketch = jnp.dot(sketch_op, slab, precision=highest, preferred_element_type=jnp.float32)
    sketch = lax.psum(partial_sketch, "row")
    finished = jnp.zeros((local_width,), dtype=bool)
    factor_parts = []
    for panel_number in range(pivots.shape[0]):
        block_start = block_order[panel_number] * panel_width
        owner_col = block_start // local_width
        block_offset = block_start - owner_col * local_width
        owns_block = col_place == owner_col
        pivot_list = pivots[panel_number]
        local_index = pivot_list - col_base
        selector = (
            jnp.arange(local_width, dtype=jnp.int32)[:, None] == local_index[None, :]
        ).astype(jnp.float32)
        targeted = jnp.sum(selector, axis=1) > 0.5
        picked = jnp.dot(slab, selector, precision=highest, preferred_element_type=jnp.float32)
        picked_sketch = jnp.dot(
            sketch, selector, precision=highest, preferred_element_type=jnp.float32
        )
        own_block = lax.dynamic_slice_in_dim(slab, block_offset, panel_width, 1)
        own_sketch = lax.dynamic_slice_in_dim(sketch, block_offset, panel_width, 1)
        panel_cols, panel_sketch = lax.psum((picked, picked_sketch), "col")
        displaced, displaced_sketch = (
            from_root(own_block, "col", owner_col),
            from_root(own_sketch, "col", owner_col),
        )
        slab = lax.dynamic_update_slice_in_dim(
            slab, jnp.where(owns_block, panel_cols, own_block), block_offset, 1
        )
        placed = lax.dot_general(
            displaced,
            selector,
            (((1,), (1,)), ((), ())),
            precision=highest,
            preferred_element_type=jnp.float32,
        )
        slab = jnp.where(targeted[None, :], placed, slab)
        placed_sketch = lax.dot_general(
            displaced_sketch,
            selector,
            (((1,), (1,)), ((), ())),
            precision=highest,
            preferred_element_type=jnp.float32,
        )
        sketch = jnp.where(targeted[None, :], placed_sketch, sketch)
        gram_matrix = lax.psum(contract_rows(panel_cols, panel_cols), "row")
        lower_factor = jnp.linalg.cholesky(gram_matrix)
        ortho_basis = right_solve(lower_factor, panel_cols)
        projected = lax.psum(contract_rows(ortho_basis, slab), "row")
        in_block = local_cols // panel_width == block_order[panel_number]
        factor_parts.append(jnp.where(finished[None, :], 0.0, projected))
        finished = finished | in_block
        update = jnp.dot(
            ortho_basis, projected, precision=highest, preferred_element_type=jnp.float32
        )
        slab = jnp.where(finished[None, :], slab, slab - update)
        sketch_basis = right_solve(lower_factor, panel_sketch)
        sketch_update = jnp.dot(
            sketch_basis, projected, precision=highest, preferred_element_type=jnp.float32
        )
        sketch = jnp.where(finished[None, :], 0.0, sketch - sketch_update)
    return (slab, jnp.concatenate(factor_parts, axis=0), sketch)


def solution(mesh):
    return jax.shard_map(
        local,
        mesh=mesh,
        in_specs=(P("row", "col"), P(None, "row"), P(), P()),
        out_specs=(P("row", "col"), P(None, "col"), P(None, "col")),
        check_vma=False,
    )
```

profile of v0, /device:TPU:1, one launch (start us, length us, event | category | flops | bytes accessed | tf_op | source)
XLA Modules:
  0.0 1056.3 jit_solution(7208083732617475073)
XLA Ops:
  7.2 2.3 copy.36
  9.6 2.0 copy-done.1
  11.6 4.5 fusion.31
  17.5 2.3 dynamic-slice_select_fusion.1
  19.7 5.2 convolution_bitcast_fusion
  24.9 118.8 %all-reduce.18.cloned.1.call-done = f32[256,512]{1,0:T(8,128)} async-done(((f32[256,512]{1,0:T(8,128)}), f32[256,512]{1,0:T(8,128)}) %all-reduce.18.cloned.1.call-update) | async-done | bytes 524304 | tf_op jit(solution)/shard_map/psum | solution.py:36
  143.7 2.1 fusion.4
  145.8 1.6 dynamic-slice_select_fusion.3
  147.6 154.5 %all-reduce.22.cloned.1.call-done = (f32[2048,128]{1,0:T(8,128)}, f32[2048,128]{1,0:T(8,128)}, f32[256,128]{1,0:T(8,128)}, f32[256,128]{1,0:T(8,128)}) async-done(((f32[2048,128]{1,0:T(8,128)}, f32[2048,128]{1,0:T(8,128)}, f32[256,128]{1,0:T(8,128)}, f32[256,128]{1,0:T(8,128)}), (f32[2048,128]{1,0:T(8,128)}, f32[2048,128]{1,0:T(8,128)}, f32[256,128]{1,0:T(8,128)}, ...) | async-done | bytes 2359312 | tf_op jit(solution)/shard_map/psum | solution.py:56
  302.0 2.4 select_dynamic-update-slice_fusion.1
  304.4 2.4 fusion.27
  307.1 6.3 convolution_select_fusion.1
  313.5 113.2 %all-reduce.10.cloned.1.call-done = f32[128,128]{0,1:T(8,128)} async-done(((f32[128,128]{0,1:T(8,128)}), f32[128,128]{0,1:T(8,128)}) %all-reduce.10.cloned.1.call-update) | async-done | bytes 65552 | tf_op jit(solution)/shard_map/psum | solution.py:80
  428.5 11.7 %cholesky.44 = f32[128,128]{1,0:T(8,128)S(1)} custom-call(f32[128,128]{1,0:T(8,128)S(1)} %fusion.22), custom_call_target="Cholesky" | custom-call | tf_op jit(solution)/shard_map/jit(cholesky)/cholesky | solution.py:81
  441.5 9.8 custom-call.10
  453.4 5.3 fusion.28
  460.7 124.1 %all-reduce.12.cloned.1.call-done = f32[128,512]{1,0:T(8,128)} async-done(((f32[128,512]{1,0:T(8,128)}), f32[128,512]{1,0:T(8,128)}) %all-reduce.12.cloned.1.call-update) | async-done | bytes 262160 | tf_op jit(solution)/shard_map/psum | solution.py:83
  584.8 1.6 fusion.32
  586.3 1.6 fusion.1
  589.0 5.5 subtract_select_fusion.1
  594.5 3.0 fusion.6
  599.5 154.4 %all-reduce.20.cloned.1.call-done = (f32[2048,128]{1,0:T(8,128)}, f32[2048,128]{1,0:T(8,128)}, f32[256,128]{1,0:T(8,128)}, f32[256,128]{1,0:T(8,128)}) async-done(((f32[2048,128]{1,0:T(8,128)}, f32[2048,128]{1,0:T(8,128)}, f32[256,128]{1,0:T(8,128)}, f32[256,128]{1,0:T(8,128)}), (f32[2048,128]{1,0:T(8,128)}, f32[2048,128]{1,0:T(8,128)}, f32[256,128]{1,0:T(8,128)}, ...) | async-done | bytes 2359312 | tf_op jit(solution)/shard_map/psum | solution.py:56
  753.9 2.4 select_dynamic-update-slice_fusion
  756.3 2.4 fusion.29
  759.1 6.3 convolution_select_fusion
  765.4 113.1 %all-reduce.14.cloned.1.call-done = f32[128,128]{0,1:T(8,128)} async-done(((f32[128,128]{0,1:T(8,128)}), f32[128,128]{0,1:T(8,128)}) %all-reduce.14.cloned.1.call-update) | async-done | bytes 65552 | tf_op jit(solution)/shard_map/psum | solution.py:80
  880.4 11.7 %cholesky.55 = f32[128,128]{1,0:T(8,128)S(1)} custom-call(f32[128,128]{1,0:T(8,128)S(1)} %fusion.19), custom_call_target="Cholesky" | custom-call | tf_op jit(solution)/shard_map/jit(cholesky)/cholesky | solution.py:81
  893.4 9.8 custom-call.11
  905.3 5.4 fusion.30
  912.3 124.4 %all-reduce.16.cloned.1.call-done = f32[128,512]{1,0:T(8,128)} async-done(((f32[128,512]{1,0:T(8,128)}), f32[128,512]{1,0:T(8,128)}) %all-reduce.16.cloned.1.call-update) | async-done | bytes 262160 | tf_op jit(solution)/shard_map/psum | solution.py:83
  1036.7 1.9 fusion.33
  1039.9 8.2 subtract_select_fusion
  (75 shorter events, 19.9 us)
Async XLA Ops:
  7.2 4.4 copy-start
  7.2 136.5 %all-reduce.18.cloned.1.call-start = ((), (), s32[]{:S(2)}) async-start(), calls=%async_computation.4 | async-start | bytes 1048576 | tf_op jit(solution)/shard_map/psum | solution.py:36
  9.6 2.0 copy-start.1
  11.6 4.6 copy-start.15
  11.6 8.2 copy-start.16
  16.1 286.0 %all-reduce.22.cloned.1.call-start = ((), (), s32[]{:S(2)}) async-start(), calls=%async_computation.6 | async-start | bytes 4718592 | tf_op jit(solution)/shard_map/psum | solution.py:56
  147.4 279.2 %all-reduce.10.cloned.1.call-start = ((), (), s32[]{:S(2)}) async-start(), calls=%async_computation | async-start | bytes 131072 | tf_op jit(solution)/shard_map/psum | solution.py:80
  302.0 2.4 copy-start.3
  306.9 277.8 %all-reduce.12.cloned.1.call-start = ((), (), s32[]{:S(2)}) async-start(), calls=%async_computation.1 | async-start | bytes 524288 | tf_op jit(solution)/shard_map/psum | solution.py:83
  427.6 32.8 %copy-start.12 = (f32[256,128]{1,0:T(8,128)S(1)}, f32[256,128]{1,0:T(8,128)}, u32[]{:S(2)}) copy-start(f32[256,128]{1,0:T(8,128)} %get-tuple-element.12) | copy-start | bytes 393220
  452.4 1.0 copy-start.5
  458.7 130.3 %copy-start.6 = (f32[2048,128]{0,1:T(8,128)S(1)}, f32[2048,128]{0,1:T(8,128)}, u32[]{:S(2)}) copy-start(f32[2048,128]{0,1:T(8,128)} %copy-done.5) | copy-start | bytes 3145732
  458.8 295.2 %all-reduce.20.cloned.1.call-start = ((), (), s32[]{:S(2)}) async-start(), calls=%async_computation.5 | async-start | bytes 4718592 | tf_op jit(solution)/shard_map/psum | solution.py:56
  587.9 9.6 copy-start.8
  594.5 3.7 copy-start.2
  599.3 279.2 %all-reduce.14.cloned.1.call-start = ((), (), s32[]{:S(2)}) async-start(), calls=%async_computation.2 | async-start | bytes 131072 | tf_op jit(solution)/shard_map/psum | solution.py:80
  753.9 2.4 copy-start.4
  758.8 277.9 %all-reduce.16.cloned.1.call-start = ((), (), s32[]{:S(2)}) async-start(), calls=%async_computation.3 | async-start | bytes 524288 | tf_op jit(solution)/shard_map/psum | solution.py:83
  879.5 32.5 %copy-start.13 = (f32[256,128]{1,0:T(8,128)S(1)}, f32[256,128]{1,0:T(8,128)}, u32[]{:S(2)}) copy-start(f32[256,128]{1,0:T(8,128)} %get-tuple-element.8) | copy-start | bytes 393220
  903.2 135.4 %copy-start.14 = (f32[256,128]{1,0:T(8,128)S(1)}, f32[256,128]{1,0:T(8,128)}, u32[]{:S(2)}) copy-start(f32[256,128]{1,0:T(8,128)} %get-tuple-element.9) | copy-start | bytes 393220
  904.3 1.0 copy-start.7
  905.3 133.3 %copy-start.9 = (f32[256,512]{1,0:T(8,128)S(1)}, f32[256,512]{1,0:T(8,128)}, u32[]{:S(2)}) copy-start(f32[256,512]{1,0:T(8,128)} %copy-done.8) | copy-start | bytes 1572868
  1039.9 8.2 copy-start.10
  1039.9 8.2 copy-start.11
Sparse Core Ops, SparseCore 0:
  16.2 127.4 all-reduce.17
  147.5 154.4 all-reduce.21
  307.0 119.5 all-reduce.9
  458.9 125.8 all-reduce.11
  599.4 154.4 all-reduce.19
  758.9 119.5 all-reduce.13
  910.8 125.8 all-reduce.15
where the time goes:
time: 1060 us
  waiting for transfers between devices  902 us (85%)
  matrix products  66.9 us (6%)
  other arithmetic  61 us (6%)
  between operations  16.2 us (2%)
    psum x2, waiting for transfers between devices, local(): panel_cols, panel_sketch = lax.psum((picked, picked_sketch), 'col')  309 us
    psum x2, waiting for transfers between devices, local(): projected = lax.psum(contract_rows(ortho_basis, slab), 'row')  248 us
    psum x2, waiting for transfers between devices, local(): gram_matrix = lax.psum(contract_rows(panel_cols, panel_cols), 'row')  226 us
    psum x1, waiting for transfers between devices, local(): sketch = lax.psum(partial_sketch, 'row')  119 us
    another operation x6, other arithmetic, local(): lower_factor = jnp.linalg.cholesky(gram_matrix)  24.8 us
  transfers between devices with their start and end apart: 7, of which 7 were waited for; matrix products, arithmetic and copies ran while one was open for 2% of the time, Pallas kernels for 0%

commit v1 on v0

--- a/solution.py
+++ b/solution.py
@@ -80,7 +80,7 @@
         gram_matrix = lax.psum(contract_rows(panel_cols, panel_cols), "row")
         lower_factor = jnp.linalg.cholesky(gram_matrix)
         ortho_basis = right_solve(lower_factor, panel_cols)
-        projected = lax.psum(contract_rows(ortho_basis, slab), "row")
+        projected = jnp.sum(lax.all_gather(contract_rows(ortho_basis, slab), "row"), axis=0)
         in_block = local_cols // panel_width == block_order[panel_number]
         factor_parts.append(jnp.where(finished[None, :], 0.0, projected))
         finished = finished | in_block

time: 1060 us -> 897 us (0.85)
  waiting for transfers between devices: 902 us -> 735 us
    psum x2 -> x0, waiting for transfers between devices: 248 us -> none  [local(): projected = lax.psum(contract_rows(ortho_basis, slab), 'row')]
    all_gather x0 -> x2, waiting for transfers between devices: none -> 83.3 us  [local(): lax.all_gather(contract_rows(ortho_basis, slab), 'row')]
  transfers between devices with their start and end apart: 7 -> 7, of which waited for: 7 -> 7; matrix products, arithmetic and copies ran while one was open for 2% -> 3% of each run, Pallas kernels for 0% -> 0%
where the time goes in v1:
time: 897 us; the launch traced here: 890 us
  waiting for transfers between devices  735 us (82%)
  other arithmetic  66.6 us (7%)
  matrix products  62.1 us (7%)
  between operations  16.2 us (2%)
    psum x2, waiting for transfers between devices, local(): panel_cols, panel_sketch = lax.psum((picked, picked_sketch), 'col')  307 us
    psum x2, waiting for transfers between devices, local(): gram_matrix = lax.psum(contract_rows(panel_cols, panel_cols), 'row')  226 us
    psum x1, waiting for transfers between devices, local(): sketch = lax.psum(partial_sketch, 'row')  119 us
    all_gather x2, waiting for transfers between devices, local(): lax.all_gather(contract_rows(ortho_basis, slab), 'row')  83.3 us
    another operation x6, other arithmetic, local(): lower_factor = jnp.linalg.cholesky(gram_matrix)  24.8 us
    another operation x4, other arithmetic, right_solve(): lax.linalg.triangular_solve(lower_factor, values, left_side=False, lower=...  20.9 us
  transfers between devices with their start and end apart: 7, of which 7 were waited for; matrix products, arithmetic and copies ran while one was open for 3% of the time, Pallas kernels for 0%

profile of v1, /device:TPU:1, one launch (start us, length us, event | category | flops | bytes accessed | tf_op | source)
XLA Modules:
  0.0 889.8 jit_solution(7334969142407811742)
XLA Ops:
  7.2 2.3 copy.34
  9.6 2.0 copy-done.1
  11.6 4.5 fusion.31
  17.5 2.3 dynamic-slice_select_fusion.1
  19.8 5.2 convolution_bitcast_fusion
  24.9 118.8 %all-reduce.12.cloned.1.call-done = f32[256,512]{1,0:T(8,128)} async-done(((f32[256,512]{1,0:T(8,128)}), f32[256,512]{1,0:T(8,128)}) %all-reduce.12.cloned.1.call-update) | async-done | bytes 524304 | tf_op jit(solution)/shard_map/psum | solution.py:36
  143.7 2.1 fusion.4
  145.8 1.6 dynamic-slice_select_fusion.3
  148.2 153.8 %all-reduce.16.cloned.1.call-done = (f32[2048,128]{1,0:T(8,128)}, f32[2048,128]{1,0:T(8,128)}, f32[256,128]{1,0:T(8,128)}, f32[256,128]{1,0:T(8,128)}) async-done(((f32[2048,128]{1,0:T(8,128)}, f32[2048,128]{1,0:T(8,128)}, f32[256,128]{1,0:T(8,128)}, f32[256,128]{1,0:T(8,128)}), (f32[2048,128]{1,0:T(8,128)}, f32[2048,128]{1,0:T(8,128)}, f32[256,128]{1,0:T(8,128)}, ...) | async-done | bytes 2359312 | tf_op jit(solution)/shard_map/psum | solution.py:56
  302.0 2.4 select_dynamic-update-slice_fusion.1
  304.4 2.4 fusion.27
  307.5 6.3 convolution_select_fusion.1
  313.8 112.8 %all-reduce.8.cloned.1.call-done = f32[128,128]{0,1:T(8,128)} async-done(((f32[128,128]{0,1:T(8,128)}), f32[128,128]{0,1:T(8,128)}) %all-reduce.8.cloned.1.call-update) | async-done | bytes 65552 | tf_op jit(solution)/shard_map/psum | solution.py:80
  428.5 11.7 %cholesky.44 = f32[128,128]{1,0:T(8,128)S(1)} custom-call(f32[128,128]{1,0:T(8,128)S(1)} %fusion.22), custom_call_target="Cholesky" | custom-call | tf_op jit(solution)/shard_map/jit(cholesky)/cholesky | solution.py:81
  441.5 9.8 %custom-call.10 = f32[1,128,128]{1,2,0:T(8,128)S(1)} custom-call(f32[1,128,128]{2,1,0:T(8,128)S(1)} %fusion.15), custom_call_target="InvertDiagBlocksLowerTriangular" | custom-call | tf_op jit(solution)/shard_map/triangular_solve/custom-call.0 | solution.py:23
  453.4 5.3 fusion.28
  460.0 41.8 %all-gather.5.cloned.1.call-done = f32[2048,512]{1,0:T(8,128)} async-done(((f32[128,512]{1,0:T(8,128)}), f32[2048,512]{1,0:T(8,128)}) %all-gather.5.cloned.1.call-update) | async-done | bytes 4194320 | tf_op jit(solution)/shard_map/all_gather | solution.py:83
  501.9 2.6 reduce_sum.38
  504.5 5.6 subtract_select_fusion.1
  512.3 3.0 fusion.6
  517.4 153.0 %all-reduce.14.cloned.1.call-done = (f32[2048,128]{1,0:T(8,128)}, f32[2048,128]{1,0:T(8,128)}, f32[256,128]{1,0:T(8,128)}, f32[256,128]{1,0:T(8,128)}) async-done(((f32[2048,128]{1,0:T(8,128)}, f32[2048,128]{1,0:T(8,128)}, f32[256,128]{1,0:T(8,128)}, f32[256,128]{1,0:T(8,128)}), (f32[2048,128]{1,0:T(8,128)}, f32[2048,128]{1,0:T(8,128)}, f32[256,128]{1,0:T(8,128)}, ...) | async-done | bytes 2359312 | tf_op jit(solution)/shard_map/psum | solution.py:56
  670.4 2.4 select_dynamic-update-slice_fusion
  672.8 2.4 fusion.29
  675.5 6.3 convolution_select_fusion
  681.9 113.1 %all-reduce.10.cloned.1.call-done = f32[128,128]{0,1:T(8,128)} async-done(((f32[128,128]{0,1:T(8,128)}), f32[128,128]{0,1:T(8,128)}) %all-reduce.10.cloned.1.call-update) | async-done | bytes 65552 | tf_op jit(solution)/shard_map/psum | solution.py:80
  796.8 11.7 %cholesky.55 = f32[128,128]{1,0:T(8,128)S(1)} custom-call(f32[128,128]{1,0:T(8,128)S(1)} %fusion.19), custom_call_target="Cholesky" | custom-call | tf_op jit(solution)/shard_map/jit(cholesky)/cholesky | solution.py:81
  809.9 9.8 %custom-call.11 = f32[1,128,128]{1,2,0:T(8,128)S(1)} custom-call(f32[1,128,128]{2,1,0:T(8,128)S(1)} %fusion.16), custom_call_target="InvertDiagBlocksLowerTriangular" | custom-call | tf_op jit(solution)/shard_map/triangular_solve/custom-call.0 | solution.py:23
  821.7 5.3 fusion.30
  827.1 1.4 compare_or_fusion
  828.8 41.4 %all-gather.7.cloned.1.call-done = f32[2048,512]{1,0:T(8,128)} async-done(((f32[128,512]{1,0:T(8,128)}), f32[2048,512]{1,0:T(8,128)}) %all-gather.7.cloned.1.call-update) | async-done | bytes 4194320 | tf_op jit(solution)/shard_map/all_gather | solution.py:83
  870.2 2.9 reduce_sum.39
  873.2 6.8 subtract_select_fusion
  (82 shorter events, 20.6 us)
Async XLA Ops:
  7.2 4.4 copy-start
  7.2 136.5 %all-reduce.12.cloned.1.call-start = ((), (), s32[]{:S(2)}) async-start(), calls=%async_computation.2 | async-start | bytes 1048576 | tf_op jit(solution)/shard_map/psum | solution.py:36
  9.6 2.0 copy-start.1
  11.6 4.6 copy-start.18
  11.6 8.2 copy-start.19
  16.1 286.0 %all-reduce.16.cloned.1.call-start = ((), (), s32[]{:S(2)}) async-start(), calls=%async_computation.6 | async-start | bytes 4718592 | tf_op jit(solution)/shard_map/psum | solution.py:56
  147.4 279.2 %all-reduce.8.cloned.1.call-start = ((), (), s32[]{:S(2)}) async-start(), calls=%async_computation | async-start | bytes 131072 | tf_op jit(solution)/shard_map/psum | solution.py:80
  302.0 2.4 copy-start.3
  306.9 195.0 %all-gather.5.cloned.1.call-start = ((), (), s32[]{:S(2)}) async-start(), calls=%async_computation.3 | async-start | bytes 4456448 | tf_op jit(solution)/shard_map/all_gather | solution.py:83
  427.6 32.1 %copy-start.14 = (f32[256,128]{1,0:T(8,128)S(1)}, f32[256,128]{1,0:T(8,128)}, u32[]{:S(2)}) copy-start(f32[256,128]{1,0:T(8,128)} %get-tuple-element.12) | copy-start | bytes 393220
  452.4 1.0 copy-start.5
  458.7 45.8 %copy-start.6 = (f32[2048,128]{0,1:T(8,128)S(1)}, f32[2048,128]{0,1:T(8,128)}, u32[]{:S(2)}) copy-start(f32[2048,128]{0,1:T(8,128)} %copy-done.5) | copy-start | bytes 3145732
  458.7 211.6 %all-reduce.14.cloned.1.call-start = ((), (), s32[]{:S(2)}) async-start(), calls=%async_computation.5 | async-start | bytes 4718592 | tf_op jit(solution)/shard_map/psum | solution.py:56
  504.5 5.6 copy-start.11
  504.5 6.3 copy-start.13
  504.5 6.3 copy-start.16
  510.1 5.9 copy-start.2
  511.2 4.1 copy-start.9
  517.2 277.8 %all-reduce.10.cloned.1.call-start = ((), (), s32[]{:S(2)}) async-start(), calls=%async_computation.1 | async-start | bytes 131072 | tf_op jit(solution)/shard_map/psum | solution.py:80
  670.4 2.4 copy-start.4
  675.3 195.0 %all-gather.7.cloned.1.call-start = ((), (), s32[]{:S(2)}) async-start(), calls=%async_computation.4 | async-start | bytes 4456448 | tf_op jit(solution)/shard_map/all_gather | solution.py:83
  795.9 32.5 %copy-start.15 = (f32[256,128]{1,0:T(8,128)S(1)}, f32[256,128]{1,0:T(8,128)}, u32[]{:S(2)}) copy-start(f32[256,128]{1,0:T(8,128)} %get-tuple-element.8) | copy-start | bytes 393220
  820.8 1.0 copy-start.7
  827.1 46.1 %copy-start.8 = (f32[2048,128]{0,1:T(8,128)S(1)}, f32[2048,128]{0,1:T(8,128)}, u32[]{:S(2)}) copy-start(f32[2048,128]{0,1:T(8,128)} %copy-done.7) | copy-start | bytes 3145732
  873.2 6.8 copy-start.12
  873.2 8.2 copy-start.10
  873.2 8.2 copy-start.17
Sparse Core Ops, SparseCore 0:
  16.2 127.4 all-reduce.11
  147.5 154.4 all-reduce.15
  307.0 119.5 all-reduce.7
  458.9 42.9 all-gather.4
  517.3 153.0 all-reduce.13
  675.4 119.5 all-reduce.9
  827.2 42.9 all-gather.6
